TPU v7x, 256 devices: a whole 4x4x8 slice. The times are simulated.
256 devices in a mesh: section: 16 (over x, y), tensor: 16 (over z, core).
Axes of the slice: x: 4, y: 4, z: 8, core: 2. Of those that a mesh axis runs over, the one named last changes fastest.
Arguments:
- queries: bfloat16 [16, 512, 8192], P('section', None, 'tensor'), may hold values from -20 to 20
- key_rows: bfloat16 [16, 512, 1024], P('section'), may hold values from -6 to 6
- value_rows: bfloat16 [16, 512, 1024], P('section'), may hold values from -6 to 6
- out_grad: bfloat16 [16, 512, 8192], P('section', None, 'tensor'), may hold values from -24 to 24
- layer_input: bfloat16 [16, 512, 8192], P('section', 'tensor'), may hold values from -64 to 64
- query_weight: bfloat16 [16, 8192, 8192], P('section', None, 'tensor'), may hold values from -0.0625 to 0.0625
- dion_basis: float32 [16, 8192, 256], P('section', 'tensor'), may hold values from -0.0625 to 0.0625
- lengths: int32 [16, 3], P('section'), may hold values from 1 to 256, 512 in all within a row
Outputs:
- upstream: bfloat16 [16, 512, 8192], P('section', 'tensor')
- left_factor: float32 [16, 8192, 256], P('section', 'tensor')
- right_factor: float32 [16, 8192, 256], P('section', 'tensor')
Inputs may be any that keep to these rules, and one draw needn't show every extreme that they name: For each section the lengths of the prompt, the chosen and the rejected response, in that order, summing to 512.
All inputs are finite; a program needn't handle non-finite values.
Results may differ from a plain program's by a relative error of at most 0.022.
Values may be sent and summed in bfloat16 or wider, within the bound.
No kernel may reach another device: no remote copies, remote signals or barrier semaphores. Data moves between devices by JAX's collectives and lax.ppermute only.
A program may use at most 64 MiB of HBM per device.

v0:
```python
import math
import jax
import jax.numpy as jnp
from jax import lax
from jax.sharding import PartitionSpec as P

D = 8192
HD = 128
GROUP = 8
rope_base = 500000.0
highest = lax.Precision.HIGHEST


def shifted(value, axis, steps):
    count = lax.axis_size(axis)
    first, last = (max(0, -steps), min(count, count - steps))
    return lax.ppermute(value, axis, [(source, source + steps) for source in range(first, last)])


def tree_layout(lengths_row, token_count):
    token_ids = jnp.arange(token_count, dtype=jnp.int32)
    bound_one = lengths_row[0]
    bound_two = lengths_row[0] + lengths_row[1]
    positions = jnp.where(token_ids < bound_two, token_ids, token_ids - lengths_row[1]).astype(
        jnp.float32
    )
    row_ids = token_ids[:, None]
    col_ids = token_ids[None, :]
    crossed = (row_ids >= bound_two) & (col_ids >= bound_one) & (col_ids < bound_two)
    visible = (col_ids <= row_ids) & jnp.logical_not(crossed)
    return (positions, visible)


def unrotate(rotated, positions):
    head_dim = rotated.shape[-1]
    half_dim = head_dim // 2
    freq_ids = jnp.arange(half_dim, dtype=jnp.float32)
    inverse = jnp.exp(-math.log(rope_base) * 2.0 * freq_ids / head_dim)
    angles = positions[:, None] * inverse[None, :]
    cosine = jnp.cos(angles)[:, None, :]
    sine_part = jnp.sin(angles)[:, None, :]
    first_half = rotated[..., :half_dim]
    second_half = rotated[..., half_dim:]
    return jnp.concatenate(
        [
            first_half * cosine + second_half * sine_part,
            second_half * cosine - first_half * sine_part,
        ],
        axis=-1,
    )


def local_backward(query_heads, grad_heads, key_block, value_block, visible):
    score_scale = 1.0 / math.sqrt(query_heads.shape[-1])
    scores = (
        jnp.einsum("qhd,kd->hqk", query_heads, key_block, preferred_element_type=jnp.float32)
        * score_scale
    )
    scores = jnp.where(visible[None], scores, -jnp.inf)
    row_max = jnp.max(scores, axis=-1, keepdims=True)
    exp_scores = jnp.exp(scores - row_max)
    weights = exp_scores / jnp.sum(exp_scores, axis=-1, keepdims=True)
    weights_low = weights.astype(jnp.bfloat16)
    outputs = jnp.einsum(
        "hqk,kd->qhd", weights_low, value_block, preferred_element_type=jnp.float32
    )
    out_dot = jnp.sum(grad_heads.astype(jnp.float32) * outputs, axis=-1)
    prob_grad = jnp.einsum(
        "qhd,kd->hqk", grad_heads, value_block, preferred_element_type=jnp.float32
    )
    score_grad = (weights * (prob_grad - out_dot.T[:, :, None])).astype(jnp.bfloat16)
    return (
        jnp.einsum("hqk,kd->qhd", score_grad, key_block, preferred_element_type=jnp.float32)
        * score_scale
    )


def local(queries, key_rows, value_rows, out_grad, layer_input, query_weight, dion_basis, lengths):
    token_count = queries.shape[1]
    local_width = queries.shape[2]
    local_heads = local_width // HD
    tensor_count = lax.axis_size("tensor")
    tensor_index = lax.axis_index("tensor")
    col_width = D // tensor_count
    gathered = lax.all_gather(layer_input[0], "tensor", axis=0, tiled=True)
    columns = lax.dynamic_slice_in_dim(gathered, tensor_index * col_width, col_width, 1)
    positions, visible = tree_layout(lengths[0], token_count)
    group_head = tensor_index * local_heads // GROUP
    key_block = lax.dynamic_slice_in_dim(key_rows[0], group_head * HD, HD, 1)
    value_block = lax.dynamic_slice_in_dim(value_rows[0], group_head * HD, HD, 1)
    rotated = local_backward(
        queries[0].reshape(token_count, local_heads, HD),
        out_grad[0].reshape(token_count, local_heads, HD),
        key_block,
        value_block,
        visible,
    )
    query_grad = unrotate(rotated, positions).reshape(token_count, local_width).astype(jnp.bfloat16)
    weight_local = query_weight[0]
    layer_grad = lax.psum_scatter(
        lax.dot_general(
            query_grad, weight_local, (((1,), (1,)), ((), ())), preferred_element_type=jnp.float32
        ).astype(jnp.bfloat16),
        "tensor",
        scatter_dimension=0,
        tiled=True,
    )
    upstream = shifted(layer_grad, "section", -1)
    grad_wide = query_grad.astype(jnp.float32)
    projected = lax.psum(jnp.dot(grad_wide, dion_basis[0], precision=highest), "tensor")
    column_wide = columns.astype(jnp.float32)
    left_raw = lax.dot_general(column_wide, projected, (((0,), (0,)), ((), ())), precision=highest)
    gram_part = lax.dot_general(left_raw, left_raw, (((0,), (0,)), ((), ())), precision=highest)
    mixed_part = jnp.dot(column_wide, left_raw, precision=highest)
    gram_total, mixed_total = lax.psum((gram_part, mixed_part), "tensor")
    lower_factor = jnp.linalg.cholesky(gram_total)
    left_orth = lax.linalg.triangular_solve(
        lower_factor, left_raw, left_side=False, lower=True, transpose_a=True
    )
    mixed_orth = lax.linalg.triangular_solve(
        lower_factor, mixed_total, left_side=False, lower=True, transpose_a=True
    )
    right_factor = lax.dot_general(
        grad_wide, mixed_orth, (((0,), (0,)), ((), ())), precision=highest
    )
    return (upstream[None], (left_orth * math.sqrt(D))[None], right_factor[None])


def solution(mesh):
    placed = (
        P("section", None, "tensor"),
        P("section", None, None),
        P("section", None, None),
        P("section", None, "tensor"),
        P("section", "tensor", None),
        P("section", None, "tensor"),
        P("section", "tensor", None),
        P("section", None),
    )
    return jax.shard_map(
        local,
        mesh=mesh,
        in_specs=placed,
        out_specs=(
            P("section", "tensor", None),
            P("section", "tensor", None),
            P("section", "tensor", None),
        ),
        check_vma=False,
    )
```

profile of v0, /device:TPU:26, one launch (start us, length us, event | category | flops | bytes accessed | tf_op | source)
XLA Modules:
  0.0 409.4 jit_solution(8106175779800506039)
XLA Ops:
  7.2 0.0 copy-start
  7.2 0.0 all-reduce.5.cloned.1.call-start
  7.2 1.3 fusion.63
  8.6 0.6 iota_compare_fusion.5
  10.5 0.7 select_convert_fusion
  11.2 1.2 reshape_squeeze.6
  12.4 0.7 fusion.27
  13.1 0.2 fusion.14
  13.4 2.1 fusion.64
  15.5 1.9 copy-done.3
  17.4 1.4 fusion.5
  18.8 0.4 copy.25
  19.2 1.2 reshape_squeeze.7
  20.4 0.6 fusion.13
  21.0 0.1 copy.18
  21.1 3.5 fusion.12
  24.6 0.5 multiply_cosine_fusion
  25.1 0.2 multiply_add_fusion
  25.4 0.0 copy-done.1
  25.4 1.5 fusion.19
  26.9 0.0 all-reduce.5.cloned.1.call-update
  26.9 0.0 all-gather.3.cloned.1.call-start
  27.0 0.7 all-gather.3.cloned.1.call-update
  27.7 0.0 all-reduce.7.cloned.1.call-start
  27.7 111.7 %all-reduce.5.cloned.1.call-done = f32[512,256]{1,0:T(8,128)} async-done(((f32[512,256]{1,0:T(8,128)}), f32[512,256]{1,0:T(8,128)}) %all-reduce.5.cloned.1.call-update) | async-done | bytes 524304 | tf_op jit(solution)/shard_map/psum | solution.py:110
  139.4 58.2 %all-gather.3.cloned.1.call-done = bf16[1,512,8192]{2,1,0:T(8,128)(2,1)} async-done(((bf16[1,32,8192]{2,1,0:T(8,128)(2,1)}), bf16[1,512,8192]{2,1,0:T(8,128)(2,1)}) %all-gather.3.cloned.1.call-update) | async-done | bytes 8388624 | tf_op jit(solution)/shard_map/all_gather | solution.py:85
  197.7 1.9 fusion.23
  199.6 1.7 fusion.65
  201.3 2.5 fusion.21
  203.8 0.0 all-reduce.7.cloned.1.call-update
  203.8 0.0 reduce-scatter.2.cloned.1.call-start
  203.9 10.2 %convolution_convert_fusion = bf16[512,8192]{1,0:T(8,128)(2,1)} fusion(bf16[512,512]{0,1:T(8,128)(2,1)S(1)} %bitcast.114, bf16[1,8192,512]{2,1,0:T(8,128)(2,1)} %param.15), kind=kOutput, calls=%fused_computation.3 | convolution fusion | flops 4299161600 | bytes 17301504 | tf_op jit(solution)/shard_map/dot_general | solution.py:101
  214.1 0.0 reduce-scatter.2.cloned.1.call-update
  214.1 99.1 %all-reduce.7.cloned.1.call-done = (f32[256,256]{0,1:T(8,128)}, f32[512,256]{1,0:T(8,128)}) async-done(((f32[256,256]{0,1:T(8,128)}, f32[512,256]{1,0:T(8,128)}), (f32[256,256]{0,1:T(8,128)}, f32[512,256]{1,0:T(8,128)})) %all-reduce.7.cloned.1.call-update) | async-done | bytes 786448 | tf_op jit(solution)/shard_map/psum | solution.py:115
  313.3 1.1 copy.22
  314.4 1.0 fusion.35
  315.4 11.7 %cholesky.50 = f32[128,128]{1,0:T(8,128)S(1)} custom-call(f32[128,128]{1,0:T(8,128)S(1)} %cholesky.118), custom_call_target="Cholesky" | custom-call | tf_op jit(solution)/shard_map/jit(cholesky)/cholesky | solution.py:116
  327.2 9.8 %custom-call.14 = f32[1,128,128]{1,2,0:T(8,128)S(1)} custom-call(f32[1,128,128]{2,1,0:T(8,128)S(1)} %get-tuple-element.43), custom_call_target="InvertDiagBlocksLowerTriangular" | custom-call | tf_op jit(solution)/shard_map/jit(cholesky)/cholesky | solution.py:116
  337.0 0.2 constant_dynamic-update-slice_fusion
  337.2 0.3 convolution_subtract_fusion.2
  337.5 11.7 %cholesky.105 = f32[128,128]{1,0:T(8,128)S(1)} custom-call(f32[128,128]{1,0:T(8,128)S(1)} %convolution_subtract_fusion.2), custom_call_target="Cholesky" | custom-call | tf_op jit(solution)/shard_map/jit(cholesky)/cholesky | solution.py:116
  349.2 0.6 compare_reduce_fusion
  349.9 0.6 compare_reduce_fusion.1
  351.9 0.1 broadcast.214
  351.9 4.0 while.4
  351.9 0.6 fusion.80
  352.5 1.4 bitcast_dynamic-update-slice_fusion.2
  353.9 0.6 fusion.80
  354.5 1.4 bitcast_dynamic-update-slice_fusion.2
  355.9 19.9 %custom-call.16 = f32[2,128,128]{1,2,0:T(8,128)S(1)} custom-call(f32[2,128,128]{2,1,0:T(8,128)S(1)} %get-tuple-element.18), custom_call_target="InvertDiagBlocksLowerTriangular" | custom-call | tf_op jit(solution)/shard_map/triangular_solve/custom-call.0 | solution.py:117
  375.8 0.4 fusion.33
  376.2 0.6 convolution_subtract_fusion.1
  376.8 0.4 fusion.50
  377.3 0.1 fusion.15
  377.3 1.0 copy.23
  378.3 0.0 copy-done.2
  378.3 0.4 fusion.31
  378.8 8.2 %reduce-scatter.2.cloned.1.call-done = bf16[32,8192]{1,0:T(8,128)(2,1)} async-done(((bf16[512,8192]{1,0:T(8,128)(2,1)}), bf16[32,8192]{1,0:T(8,128)(2,1)}) %reduce-scatter.2.cloned.1.call-update) | async-done | bytes 524304 | tf_op jit(solution)/shard_map/reduce_scatter | solution.py:100
  387.0 2.8 collective-permute-start
  389.8 0.6 convolution_subtract_fusion
  390.4 0.4 fusion.49
  390.8 1.4 convolution_bitcast_fusion
  392.2 9.8 %collective-permute-done = bf16[32,8192]{1,0:T(8,128)(2,1)S(1)} collective-permute-done((bf16[32,8192]{1,0:T(8,128)(2,1)}, bf16[32,8192]{1,0:T(8,128)(2,1)S(1)}, u32[]{:S(2)}, u32[]{:S(2)}) %collective-permute-start) | collective-permute-done | bytes 524320 | tf_op jit(solution)/shard_map/ppermute | solution.py:17
  402.1 0.8 copy.50
  (16 shorter events, 0.2 us)
Async XLA Ops:
  7.2 5.2 %copy-start = (bf16[1,512,1024]{2,1,0:T(8,128)(2,1)S(1)}, bf16[1,512,1024]{2,1,0:T(8,128)(2,1)}, u32[]{:S(2)}) copy-start(bf16[1,512,1024]{2,1,0:T(8,128)(2,1)} %param.11) | copy-start | bytes 3145732
  7.2 132.2 %all-reduce.5.cloned.1.call-start = ((), (), s32[]{:S(2)}) async-start(), calls=%async_computation.2 | async-start | bytes 1048576 | tf_op jit(solution)/shard_map/psum | solution.py:110
  15.5 1.9 copy-start.3
  21.1 4.2 %copy-start.1 = (f32[1,512,256]{2,1,0:T(8,128)S(1)}, f32[1,512,256]{2,1,0:T(8,128)}, u32[]{:S(2)}) copy-start(f32[1,512,256]{2,1,0:T(8,128)} %param.16) | copy-start | bytes 1572868
  26.9 170.7 %all-gather.3.cloned.1.call-start = ((), (), s32[]{:S(2)}) async-start(), calls=%async_computation.3 | async-start | bytes 8912896 | tf_op jit(solution)/shard_map/all_gather | solution.py:85
  27.7 285.6 %all-reduce.7.cloned.1.call-start = ((), (), s32[]{:S(2)}) async-start(), calls=%async_computation.4 | async-start | bytes 1572864 | tf_op jit(solution)/shard_map/psum | solution.py:115
  203.8 183.2 %reduce-scatter.2.cloned.1.call-start = ((), (), s32[]{:S(2)}) async-start(), calls=%async_computation.1 | async-start | bytes 8912896 | tf_op jit(solution)/shard_map/reduce_scatter | solution.py:100
  313.3 65.1 %copy-start.2 = (f32[512,256]{1,0:T(8,128)S(1)}, f32[512,256]{1,0:T(8,128)}, u32[]{:S(2)}) copy-start(f32[512,256]{1,0:T(8,128)} %get-tuple-element.35) | copy-start | bytes 1572868
  387.0 15.1 %collective-permute-start = (bf16[32,8192]{1,0:T(8,128)(2,1)}, bf16[32,8192]{1,0:T(8,128)(2,1)S(1)}, u32[]{:S(2)}, u32[]{:S(2)}) collective-permute-start(bf16[32,8192]{1,0:T(8,128)(2,1)} %reduce-scatter.2.cloned.1.call-done), channel_id=1, source_target_pairs={{16,0},{32,16},{48,32},{64,48},{80,64},{96,80},{112,96},{128,112},... | collective-permute-start | bytes 1572872 | tf_op jit(solution)/shard_map/ppermute | solution.py:17
Sparse Core Ops, SparseCore 0:
  27.1 112.3 all-reduce.4
  141.4 56.2 all-gather.2
  203.9 109.2 all-reduce.6
  315.7 71.2 reduce-scatter.1
where the time goes:
time: 410 us; the launch traced here: 409 us
  waiting for transfers between devices  288 us (70%)
  other arithmetic  60.6 us (15%)
  matrix products  28.2 us (7%)
  between operations  16.7 us (4%)
  local copies, waits for them, and re-layouts  13.1 us (3%)
    psum x1, waiting for transfers between devices, local(): lax.psum(jnp.dot(grad_wide, dion_basis[0], precision=highest), 'tensor')  112 us
    psum x1, waiting for transfers between devices, local(): gram_total, mixed_total = lax.psum((gram_part, mixed_part), 'tensor')  99.1 us
    all_gather x1, waiting for transfers between devices, local(): gathered = lax.all_gather(layer_input[0], 'tensor', axis=0, tiled=True)  58.2 us
    another operation x7, other arithmetic, local(): lower_factor = jnp.linalg.cholesky(gram_total)  34.6 us
    another operation x4, other arithmetic, local(): lax.linalg.triangular_solve(lower_factor, left_raw, left_side=False, lowe...  19.9 us
    dot_general x1, matrix products, local(): lax.dot_general(query_grad, weight_local, (((1,), (1,)), ((), ())), prefe...  10.2 us
    ppermute x1, waiting for transfers between devices, shifted(): lax.ppermute(value, axis, [(source, source + steps) for source in range(f...  9.81 us
    reduce_scatter x1, waiting for transfers between devices, local(): lax.psum_scatter(lax.dot_general(query_grad, weight_local, (((1,), (1,)),...  8.25 us
  transfers between devices with their start and end apart: 5, of which 5 were waited for; matrix products, arithmetic and copies ran while one was open for 19% of the time, Pallas kernels for 0%

commit v1 on v0

--- a/solution.py
+++ b/solution.py
@@ -107,7 +107,9 @@
     )
     upstream = shifted(layer_grad, "section", -1)
     grad_wide = query_grad.astype(jnp.float32)
-    projected = lax.psum(jnp.dot(grad_wide, dion_basis[0], precision=highest), "tensor")
+    x = jnp.dot(grad_wide, dion_basis[0], precision=highest)
+    shards = lax.all_gather(x, "tensor")
+    projected = jnp.sum(shards, axis=0)
     column_wide = columns.astype(jnp.float32)
     left_raw = lax.dot_general(column_wide, projected, (((0,), (0,)), ((), ())), precision=highest)
     gram_part = lax.dot_general(left_raw, left_raw, (((0,), (0,)), ((), ())), precision=highest)

time: 410 us -> 355 us (0.87)
  waiting for transfers between devices: 288 us -> 229 us
    psum x1 -> x0, waiting for transfers between devices: 112 us -> none  [local(): lax.psum(jnp.dot(grad_wide, dion_basis[0], precision=highest), 'tensor')]
    all_gather x0 -> x1, waiting for transfers between devices: none -> 58 us  [local(): shards = lax.all_gather(x, 'tensor')]
    all_gather x1, waiting for transfers between devices: 58.2 us -> 52.3 us  [local(): gathered = lax.all_gather(layer_input[0], 'tensor', axis=0, tiled=True)]
  transfers between devices with their start and end apart: 5 -> 5, of which waited for: 5 -> 5; matrix products, arithmetic and copies ran while one was open for 19% -> 23% of each run, Pallas kernels for 0% -> 0%
where the time goes in v1:
time: 355 us; the launch traced here: 354 us
  waiting for transfers between devices  229 us (65%)
  other arithmetic  64.6 us (18%)
  matrix products  28 us (8%)
  between operations  16.7 us (5%)
  local copies, waits for them, and re-layouts  13.1 us (4%)
    psum x1, waiting for transfers between devices, local(): gram_total, mixed_total = lax.psum((gram_part, mixed_part), 'tensor')  99.3 us
    all_gather x1, waiting for transfers between devices, local(): shards = lax.all_gather(x, 'tensor')  58 us
    all_gather x1, waiting for transfers between devices, local(): gathered = lax.all_gather(layer_input[0], 'tensor', axis=0, tiled=True)  52.3 us
    another operation x7, other arithmetic, local(): lower_factor = jnp.linalg.cholesky(gram_total)  34.6 us
    another operation x4, other arithmetic, local(): lax.linalg.triangular_solve(lower_factor, left_raw, left_side=False, lowe...  19.9 us
    dot_general x1, matrix products, local(): lax.dot_general(query_grad, weight_local, (((1,), (1,)), ((), ())), prefe...  10.2 us
    ppermute x1, waiting for transfers between devices, shifted(): lax.ppermute(value, axis, [(source, source + steps) for source in range(f...  9.75 us
    reduce_scatter x1, waiting for transfers between devices, local(): lax.psum_scatter(lax.dot_general(query_grad, weight_local, (((1,), (1,)),...  8.64 us
  transfers between devices with their start and end apart: 5, of which 5 were waited for; matrix products, arithmetic and copies ran while one was open for 23% of the time, Pallas kernels for 0%

profile of v1, /device:TPU:26, one launch (start us, length us, event | category | flops | bytes accessed | tf_op | source)
XLA Modules:
  0.0 354.1 jit_solution(5321891218017696644)
XLA Ops:
  7.2 0.0 copy-start
  7.2 0.0 all-gather.7.cloned.1.call-start
  7.2 1.3 fusion.63
  8.6 0.6 iota_compare_fusion.5
  10.5 0.7 select_convert_fusion
  11.2 1.2 reshape_squeeze.6
  12.4 0.0 copy-done
  12.4 0.7 fusion.27
  13.1 0.2 fusion.14
  13.4 2.1 fusion.64
  15.5 1.9 copy-done.3
  17.4 1.4 fusion.5
  18.8 0.4 copy.25
  19.2 1.2 reshape_squeeze.7
  20.4 0.6 fusion.13
  21.0 0.1 copy.18
  21.1 3.5 fusion.12
  24.6 0.5 multiply_cosine_fusion
  25.1 0.2 multiply_add_fusion
  25.4 1.5 fusion.19
  26.9 0.0 all-gather.7.cloned.1.call-update
  26.9 0.0 all-gather.5.cloned.1.call-start
  27.0 0.7 all-gather.5.cloned.1.call-update
  27.7 0.0 all-reduce.4.cloned.1.call-start
  27.7 58.0 %all-gather.7.cloned.1.call-done = f32[8192,256]{1,0:T(8,128)} async-done(((f32[512,256]{1,0:T(8,128)}), f32[8192,256]{1,0:T(8,128)}) %all-gather.7.cloned.1.call-update) | async-done | bytes 8388624 | tf_op jit(solution)/shard_map/all_gather | solution.py:111
  85.7 4.0 %reduce_sum.29 = f32[512,256]{1,0:T(8,128)S(1)} reduce(f32[16,512,256]{2,1,0:T(8,128)} %bitcast.114, f32[]{:T(128)} %constant.112.clone.1), dimensions={0}, to_apply=%region_4.5 | reduce | flops 1966080 | bytes 8912900 | tf_op jit(solution)/shard_map/reduce_sum | solution.py:112
  89.7 52.3 %all-gather.5.cloned.1.call-done = bf16[1,512,8192]{2,1,0:T(8,128)(2,1)} async-done(((bf16[1,32,8192]{2,1,0:T(8,128)(2,1)}), bf16[1,512,8192]{2,1,0:T(8,128)(2,1)}) %all-gather.5.cloned.1.call-update) | async-done | bytes 8388624 | tf_op jit(solution)/shard_map/all_gather | solution.py:85
  142.0 1.8 fusion.23
  143.8 1.7 fusion.65
  145.5 2.5 fusion.21
  148.0 0.0 all-reduce.4.cloned.1.call-update
  148.0 0.0 reduce-scatter.2.cloned.1.call-start
  148.1 10.2 %convolution_convert_fusion = bf16[512,8192]{1,0:T(8,128)(2,1)} fusion(bf16[512,512]{0,1:T(8,128)(2,1)S(1)} %bitcast.116, bf16[1,8192,512]{2,1,0:T(8,128)(2,1)} %param.15), kind=kOutput, calls=%fused_computation.3 | convolution fusion | flops 4299161600 | bytes 17301504 | tf_op jit(solution)/shard_map/dot_general | solution.py:101
  158.3 0.0 reduce-scatter.2.cloned.1.call-update
  158.4 99.3 %all-reduce.4.cloned.1.call-done = (f32[256,256]{0,1:T(8,128)}, f32[512,256]{1,0:T(8,128)}) async-done(((f32[256,256]{0,1:T(8,128)}, f32[512,256]{1,0:T(8,128)}), (f32[256,256]{0,1:T(8,128)}, f32[512,256]{1,0:T(8,128)})) %all-reduce.4.cloned.1.call-update) | async-done | bytes 786448 | tf_op jit(solution)/shard_map/psum | solution.py:117
  257.7 1.1 copy.22
  258.9 1.0 fusion.35
  259.9 11.7 %cholesky.50 = f32[128,128]{1,0:T(8,128)S(1)} custom-call(f32[128,128]{1,0:T(8,128)S(1)} %cholesky.118), custom_call_target="Cholesky" | custom-call | tf_op jit(solution)/shard_map/jit(cholesky)/cholesky | solution.py:118
  271.6 9.8 %custom-call.14 = f32[1,128,128]{1,2,0:T(8,128)S(1)} custom-call(f32[1,128,128]{2,1,0:T(8,128)S(1)} %get-tuple-element.43), custom_call_target="InvertDiagBlocksLowerTriangular" | custom-call | tf_op jit(solution)/shard_map/jit(cholesky)/cholesky | solution.py:118
  281.4 0.2 constant_dynamic-update-slice_fusion
  281.7 0.3 convolution_subtract_fusion.2
  281.9 11.7 %cholesky.105 = f32[128,128]{1,0:T(8,128)S(1)} custom-call(f32[128,128]{1,0:T(8,128)S(1)} %convolution_subtract_fusion.2), custom_call_target="Cholesky" | custom-call | tf_op jit(solution)/shard_map/jit(cholesky)/cholesky | solution.py:118
  293.7 0.6 compare_reduce_fusion
  294.3 0.6 compare_reduce_fusion.1
  296.3 0.1 broadcast.214
  296.4 4.0 %while.4 = (s32[]{:T(128)}, f32[256,256]{1,0:T(8,128)S(1)}, s32[2,2]{1,0:T(2,128)S(1)}, f32[2,128,128]{2,1,0:T(8,128)S(1)}, s32[]{:T(128)}) while((s32[]{:T(128)}, f32[256,256]{1,0:T(8,128)S(1)}, s32[2,2]{1,0:T(2,128)S(1)}, f32[2,128,128]{2,1,0:T(8,128)S(1)}, s32[]{:T(128)}) %tuple.38), condition=%wide.while_cond, body=%wide.while_body.sunk | while | flops 2 | bytes 131181 | solution.py:119
  296.4 0.6 fusion.80
  297.0 1.4 bitcast_dynamic-update-slice_fusion.2
  298.4 0.6 fusion.80
  299.0 1.4 bitcast_dynamic-update-slice_fusion.2
  300.4 19.9 %custom-call.16 = f32[2,128,128]{1,2,0:T(8,128)S(1)} custom-call(f32[2,128,128]{2,1,0:T(8,128)S(1)} %get-tuple-element.18), custom_call_target="InvertDiagBlocksLowerTriangular" | custom-call | tf_op jit(solution)/shard_map/triangular_solve/custom-call.0 | solution.py:119
  320.3 0.4 fusion.33
  320.7 0.6 convolution_subtract_fusion.1
  321.3 0.4 fusion.50
  321.7 0.1 fusion.15
  321.8 1.0 copy.23
  322.8 0.4 fusion.31
  323.2 8.6 %reduce-scatter.2.cloned.1.call-done = bf16[32,8192]{1,0:T(8,128)(2,1)} async-done(((bf16[512,8192]{1,0:T(8,128)(2,1)}), bf16[32,8192]{1,0:T(8,128)(2,1)}) %reduce-scatter.2.cloned.1.call-update) | async-done | bytes 524304 | tf_op jit(solution)/shard_map/reduce_scatter | solution.py:100
  331.8 2.7 collective-permute-start
  334.6 0.6 convolution_subtract_fusion
  335.2 0.4 fusion.49
  335.6 1.4 convolution_bitcast_fusion
  337.0 9.7 %collective-permute-done = bf16[32,8192]{1,0:T(8,128)(2,1)S(1)} collective-permute-done((bf16[32,8192]{1,0:T(8,128)(2,1)}, bf16[32,8192]{1,0:T(8,128)(2,1)S(1)}, u32[]{:S(2)}, u32[]{:S(2)}) %collective-permute-start) | collective-permute-done | bytes 524320 | tf_op jit(solution)/shard_map/ppermute | solution.py:17
  346.8 0.8 copy.49
  (17 shorter events, 0.2 us)
Async XLA Ops:
  7.2 5.2 %copy-start = (bf16[1,512,1024]{2,1,0:T(8,128)(2,1)S(1)}, bf16[1,512,1024]{2,1,0:T(8,128)(2,1)}, u32[]{:S(2)}) copy-start(bf16[1,512,1024]{2,1,0:T(8,128)(2,1)} %param.11) | copy-start | bytes 3145732
  7.2 78.5 %all-gather.7.cloned.1.call-start = ((), (), s32[]{:S(2)}) async-start(), calls=%async_computation.3 | async-start | bytes 8912896 | tf_op jit(solution)/shard_map/all_gather | solution.py:111
  15.5 1.9 copy-start.3
  21.1 4.2 %copy-start.1 = (f32[1,512,256]{2,1,0:T(8,128)S(1)}, f32[1,512,256]{2,1,0:T(8,128)}, u32[]{:S(2)}) copy-start(f32[1,512,256]{2,1,0:T(8,128)} %param.16) | copy-start | bytes 1572868
  26.9 115.1 %all-gather.5.cloned.1.call-start = ((), (), s32[]{:S(2)}) async-start(), calls=%async_computation.2 | async-start | bytes 8912896 | tf_op jit(solution)/shard_map/all_gather | solution.py:85
  27.7 230.0 %all-reduce.4.cloned.1.call-start = ((), (), s32[]{:S(2)}) async-start(), calls=%async_computation.4 | async-start | bytes 1572864 | tf_op jit(solution)/shard_map/psum | solution.py:117
  148.0 183.8 %reduce-scatter.2.cloned.1.call-start = ((), (), s32[]{:S(2)}) async-start(), calls=%async_computation.1 | async-start | bytes 8912896 | tf_op jit(solution)/shard_map/reduce_scatter | solution.py:100
  257.7 65.1 %copy-start.2 = (f32[512,256]{1,0:T(8,128)S(1)}, f32[512,256]{1,0:T(8,128)}, u32[]{:S(2)}) copy-start(f32[512,256]{1,0:T(8,128)} %get-tuple-element.35) | copy-start | bytes 1572868
  331.8 14.9 %collective-permute-start = (bf16[32,8192]{1,0:T(8,128)(2,1)}, bf16[32,8192]{1,0:T(8,128)(2,1)S(1)}, u32[]{:S(2)}, u32[]{:S(2)}) collective-permute-start(bf16[32,8192]{1,0:T(8,128)(2,1)} %reduce-scatter.2.cloned.1.call-done), channel_id=1, source_target_pairs={{16,0},{32,16},{48,32},{64,48},{80,64},{96,80},{112,96},{128,112},... | collective-permute-start | bytes 1572872 | tf_op jit(solution)/shard_map/ppermute | solution.py:17
Sparse Core Ops, SparseCore 0:
  27.1 58.6 all-gather.6
  87.5 54.4 all-gather.4
  148.2 109.5 all-reduce.3
  260.3 71.4 reduce-scatter.1
